TPU v7x, 256 devices: a whole 4x4x8 slice. The times are simulated.
256 devices in a mesh: seq: 64 (over x, z, core), ctx: 4 (over y).
Axes of the slice: x: 4, y: 4, z: 8, core: 2. Of those that a mesh axis runs over, the one named last changes fastest.
Arguments:
- queries: bfloat16 [4096, 8192], P(('seq', 'ctx'))
- new_token_keys: bfloat16 [4096, 1024], P(('seq', 'ctx'))
- new_token_values: bfloat16 [4096, 1024], P(('seq', 'ctx')), may hold values from -0.796875 to 0.796875
- cache_keys: bfloat16 [64, 32768, 128], P('seq', 'ctx'), as said below
- cache_values: bfloat16 [64, 32768, 128], P('seq', 'ctx'), as said below
- block_ids: int32 [64, 64, 4, 12], P('seq', None, 'ctx'), may hold values from 0 to 63, as said below
- block_counts: int32 [64, 64, 4], P('seq', None, 'ctx'), may hold values from 1 to 12, as said below
Outputs:
- attended: bfloat16 [4096, 8192], P(('seq', 'ctx'))
Inputs may be any that keep to these rules, and one draw needn't show every extreme that they name: `block_ids`: within one list of 12 entries the key blocks are distinct; only the first block_counts of them are used. `block_counts`: the most, 12, is reached in every draw. cache_keys[h] equals cache_keys[h2] where floor(h / 8) = floor(h2 / 8). cache_values[h] equals cache_values[h2] where floor(h / 8) = floor(h2 / 8).
All inputs are finite; a program needn't handle non-finite values.
Results may differ from a plain program's by a relative error of at most 0.0075.
Values may be sent and summed in bfloat16 or wider, within the bound.
A program may use at most 64 MiB of HBM per device.

v0:
```python
import math

import jax
import jax.numpy as jnp
from jax import lax
from jax.sharding import PartitionSpec as P

HEADS_PER_GROUP = 8
TILE_QUERY_ROWS = 64
KROWS = 128
KQ = 12


def merged(value, axis, join):
    pieces = jax.tree.map(lambda part: lax.all_gather(part, axis), value)
    head = jax.tree.map(lambda part: part[0], pieces)
    tail = jax.tree.map(lambda part: part[1:], pieces)
    running, _ = lax.scan(lambda running, section: (join(running, section), None), head, tail)
    return running


def expand_heads(pairs, group_size, head_size):
    row_count = pairs.shape[0]
    kv_heads = pairs.shape[1] // head_size
    dispersed = jnp.broadcast_to(
        pairs.reshape(row_count, kv_heads, 1, head_size),
        (row_count, kv_heads, group_size, head_size),
    )
    return dispersed.reshape(row_count, kv_heads * group_size * head_size)


def soft_partial(logit_scores, visible, value_tile_rows):
    top = jnp.max(jnp.where(visible, logit_scores, -jnp.inf), axis=-1)
    exponent_terms = jnp.where(visible, jnp.exp(logit_scores - top[..., None]), jnp.float32(0.0))
    totals = jnp.sum(exponent_terms, axis=-1)
    blended = jnp.einsum(
        "nst,ntw->nsw",
        exponent_terms.astype(jnp.bfloat16),
        value_tile_rows,
        preferred_element_type=jnp.float32,
    )
    return (top, totals, blended)


def join_parts(first, second):
    top = jnp.maximum(first[0], second[0])
    factor_one = jnp.exp(first[0] - top)
    factor_two = jnp.exp(second[0] - top)
    totals = first[1] * factor_one + second[1] * factor_two
    blended = first[2] * factor_one[..., None] + second[2] * factor_two[..., None]
    return (top, totals, blended)


def body(
    queries, new_token_keys, new_token_values, cache_keys, cache_values, block_ids, block_counts
):
    seq_count = lax.axis_size("seq")
    ctx_count = lax.axis_size("ctx")
    quarter = lax.axis_index("ctx")
    head_size = cache_keys.shape[2]
    group_size = HEADS_PER_GROUP
    local_rows = queries.shape[0]
    span_rows = local_rows * seq_count * ctx_count
    block_total = span_rows // TILE_QUERY_ROWS
    scaling = 1.0 / math.sqrt(head_size)
    all_queries, every_key, every_value = (
        lax.all_gather(queries, "ctx", axis=0, tiled=True),
        lax.all_gather(new_token_keys, "ctx", axis=0, tiled=True),
        lax.all_gather(new_token_values, "ctx", axis=0, tiled=True),
    )
    head_queries = lax.all_to_all(all_queries, "seq", split_axis=1, concat_axis=0, tiled=True)
    tile_keys = cache_keys[0].reshape(-1, KROWS, head_size)
    tile_values = cache_values[0].reshape(-1, KROWS, head_size)
    listed = block_ids[0, :, 0, :]
    used = block_counts[0, :, 0]
    per_step = min(block_total, max(1, 512 // TILE_QUERY_ROWS))
    step_count = block_total // per_step
    tiled_queries = head_queries.reshape(step_count, per_step, TILE_QUERY_ROWS, head_size)

    def cached_part(operands):
        query_group_block, listed_block, used_block = operands
        selected_keys = tile_keys[listed_block].reshape(per_step, KQ * KROWS, head_size)
        picked_values = tile_values[listed_block].reshape(per_step, KQ * KROWS, head_size)
        logit_scores = (
            jnp.einsum(
                "pmt,pyt->pmy", query_group_block, selected_keys, preferred_element_type=jnp.float32
            )
            * scaling
        )
        slot_ok = jnp.arange(KQ, dtype=jnp.int32)[None, :] < used_block[:, None]
        visible = jnp.repeat(slot_ok, KROWS, axis=1)[:, None, :]
        return soft_partial(logit_scores, visible, picked_values)

    tops, sums, mixes = lax.map(
        cached_part,
        (
            tiled_queries,
            listed.reshape(step_count, per_step, KQ),
            used.reshape(step_count, per_step),
        ),
    )
    head_keys, head_values = (
        lax.all_to_all(
            expand_heads(every_key, group_size, head_size),
            "seq",
            split_axis=1,
            concat_axis=0,
            tiled=True,
        ),
        lax.all_to_all(
            expand_heads(every_value, group_size, head_size),
            "seq",
            split_axis=1,
            concat_axis=0,
            tiled=True,
        ),
    )
    owned = block_total // ctx_count
    local_queries = lax.dynamic_index_in_dim(
        head_queries.reshape(owned, ctx_count, TILE_QUERY_ROWS, head_size),
        quarter,
        1,
        keepdims=False,
    )
    block_index = jnp.arange(owned, dtype=jnp.int32) * ctx_count + quarter
    key_block = block_index * TILE_QUERY_ROWS // KROWS
    zero_tile = jnp.zeros((KROWS, head_size), jnp.bfloat16)
    padded_keys = jnp.concatenate([zero_tile, head_keys]).reshape(-1, KROWS, head_size)
    padded_values = jnp.concatenate([zero_tile, head_values]).reshape(-1, KROWS, head_size)
    nearby_keys = jnp.concatenate([padded_keys[key_block], padded_keys[key_block + 1]], axis=1)
    near_values = jnp.concatenate([padded_values[key_block], padded_values[key_block + 1]], axis=1)
    positions = (key_block[:, None] - 1) * KROWS + jnp.arange(2 * KROWS, dtype=jnp.int32)[None, :]
    query_pos = (
        block_index[:, None] * TILE_QUERY_ROWS
        + jnp.arange(TILE_QUERY_ROWS, dtype=jnp.int32)[None, :]
    )
    near_ok = (positions[:, None, :] >= 0) & (positions[:, None, :] <= query_pos[:, :, None])
    near_scores = (
        jnp.einsum("pmt,pyt->pmy", local_queries, nearby_keys, preferred_element_type=jnp.float32)
        * scaling
    )
    near_part = soft_partial(near_scores, near_ok, near_values)
    tops = tops.reshape(owned, ctx_count, TILE_QUERY_ROWS)
    sums = sums.reshape(owned, ctx_count, TILE_QUERY_ROWS)
    mixes = mixes.reshape(owned, ctx_count, TILE_QUERY_ROWS, head_size)
    own_part = (
        lax.dynamic_index_in_dim(tops, quarter, 1, keepdims=False),
        lax.dynamic_index_in_dim(sums, quarter, 1, keepdims=False),
        lax.dynamic_index_in_dim(mixes, quarter, 1, keepdims=False),
    )
    joined = join_parts(own_part, near_part)
    tops = lax.dynamic_update_index_in_dim(tops, joined[0], quarter, 1).reshape(span_rows)
    sums = lax.dynamic_update_index_in_dim(sums, joined[1], quarter, 1).reshape(span_rows)
    mixes = lax.dynamic_update_index_in_dim(mixes, joined[2], quarter, 1).reshape(
        span_rows, head_size
    )
    top_all, sum_all, mix_all = merged((tops, sums, mixes), "ctx", join_parts)
    rows_sum = lax.dynamic_index_in_dim(
        sum_all.reshape(seq_count, ctx_count, local_rows), quarter, 1, keepdims=False
    )
    rows_mix = lax.dynamic_index_in_dim(
        mix_all.reshape(seq_count, ctx_count, local_rows, head_size), quarter, 1, keepdims=False
    )
    attended_rows = (
        rows_mix.reshape(seq_count * local_rows, head_size)
        / rows_sum.reshape(seq_count * local_rows, 1)
    ).astype(jnp.bfloat16)
    return lax.all_to_all(attended_rows, "seq", split_axis=0, concat_axis=1, tiled=True)


def solution(mesh):
    return jax.shard_map(
        body,
        mesh=mesh,
        in_specs=(
            P(("seq", "ctx"), None),
            P(("seq", "ctx"), None),
            P(("seq", "ctx"), None),
            P("seq", "ctx", None),
            P("seq", "ctx", None),
            P("seq", None, "ctx", None),
            P("seq", None, "ctx"),
        ),
        out_specs=P(("seq", "ctx"), None),
        check_vma=False,
    )
```

profile of v0, /device:TPU:1, one launch (start us, length us, event | category | flops | bytes accessed | tf_op | source)
XLA Modules:
  0.0 368.0 jit_solution(3221839272614560469)
XLA Ops:
  6.5 10.9 %all_gather.22 = bf16[64,1024]{1,0:T(8,128)(2,1)S(1)} all-gather(bf16[16,1024]{1,0:T(8,128)(2,1)} %param.13), channel_id=1, replica_groups=mesh['seq'=64,'ctx'=4] {'ctx'}, dimensions={0}, use_global_device_ids=true | all-gather | bytes 163840 | tf_op jit(solution)/shard_map/all_gather | solution.py:69
  18.7 14.9 %all-to-all-start.2 = ((bf16[64,64,128]{2,0,1:T(8,128)(2,1)}), bf16[64,64,128]{2,0,1:T(8,128)(2,1)S(1)}, u32[]{:S(2)}, u32[]{:S(2)}) async-start(bf16[64,64,128]{2,0,1:T(8,128)(2,1)} %bitcast.36), calls=%async_computation.2 | async-start | bytes 2097152 | tf_op jit(solution)/shard_map/all_to_all | solution.py:110
  33.7 10.0 %all_gather.19 = bf16[64,1024]{1,0:T(8,128)(2,1)S(1)} all-gather(bf16[16,1024]{1,0:T(8,128)(2,1)S(1)} %copy-done.6), channel_id=1, replica_groups=mesh['seq'=64,'ctx'=4] {'ctx'}, dimensions={0}, use_global_device_ids=true | all-gather | bytes 163840 | tf_op jit(solution)/shard_map/all_gather | solution.py:68
  43.7 18.5 %all-to-all-done.2 = bf16[64,64,128]{2,0,1:T(8,128)(2,1)S(1)} async-done(((bf16[64,64,128]{2,0,1:T(8,128)(2,1)}), bf16[64,64,128]{2,0,1:T(8,128)(2,1)S(1)}, u32[]{:S(2)}, u32[]{:S(2)}) %all-to-all-start.2) | async-done | bytes 1048608 | tf_op jit(solution)/shard_map/all_to_all | solution.py:110
  63.5 6.2 %all-to-all-start.1 = ((bf16[64,64,128]{2,0,1:T(8,128)(2,1)}), bf16[64,64,128]{2,0,1:T(8,128)(2,1)S(1)}, u32[]{:S(2)}, u32[]{:S(2)}) async-start(bf16[64,64,128]{2,0,1:T(8,128)(2,1)} %bitcast.20), calls=%async_computation.1 | async-start | bytes 2097152 | tf_op jit(solution)/shard_map/all_to_all | solution.py:103
  70.4 28.0 %all-gather.5.cloned.1.call-done = bf16[64,8192]{1,0:T(8,128)(2,1)} async-done(((bf16[16,8192]{1,0:T(8,128)(2,1)}), bf16[64,8192]{1,0:T(8,128)(2,1)}) %all-gather.5.cloned.1.call-update) | async-done | bytes 1048592 | tf_op jit(solution)/shard_map/all_gather | solution.py:67
  100.9 11.8 %all-to-all-start = ((bf16[64,64,128]{2,0,1:T(8,128)(2,1)}), bf16[64,64,128]{2,0,1:T(8,128)(2,1)}, u32[]{:S(2)}, u32[]{:S(2)}) async-start(bf16[64,64,128]{2,0,1:T(8,128)(2,1)} %copy_bitcast_fusion), calls=%async_computation | async-start | bytes 2097152 | tf_op jit(solution)/shard_map/all_to_all | solution.py:71
  121.8 19.4 %all-to-all-done = bf16[64,64,128]{2,0,1:T(8,128)(2,1)} async-done(((bf16[64,64,128]{2,0,1:T(8,128)(2,1)}), bf16[64,64,128]{2,0,1:T(8,128)(2,1)}, u32[]{:S(2)}, u32[]{:S(2)}) %all-to-all-start) | async-done | bytes 1048608 | tf_op jit(solution)/shard_map/all_to_all | solution.py:71
  141.2 89.4 %while.28 = (s32[]{:T(128)}, f32[8,8,64]{2,1,0:T(8,128)S(1)}, f32[8,8,64]{2,1,0:T(8,128)S(1)}, f32[8,8,64,128]{3,2,1,0:T(8,128)}, s32[8,8]{1,0:T(8,128)S(1)}, /*...) while((s32[]{:T(128)}, f32[8,8,64]{2,1,0:T(8,128)S(1)}, ...), condition=%wide.region_3.4_spmd, body=%wide.region_0.3_spmd.sunk | while | flops 409731456 | bytes 49757280 | solution.py:94
  141.4 2.7 gather_fusion.1
  144.1 2.7 gather_fusion
  152.5 2.7 gather_fusion.1
  155.2 2.7 gather_fusion
  163.7 2.7 gather_fusion.1
  166.4 2.7 gather_fusion
  174.9 2.7 gather_fusion.1
  177.6 2.7 gather_fusion
  186.0 2.7 gather_fusion.1
  188.8 2.7 gather_fusion
  199.9 2.7 gather_fusion
  211.1 2.7 gather_fusion
  219.6 2.7 gather_fusion.1
  222.3 2.7 gather_fusion
  235.9 9.0 %all-gather = f32[4,1,4096]{2,1,0:T(1,128)S(1)} all-gather(f32[1,1,4096]{2,1,0:T(1,128)S(1)} %reshape.331), channel_id=1, replica_groups=mesh['seq'=64,'ctx'=4] {'ctx'}, dimensions={0}, use_global_device_ids=true | all-gather | bytes 81920 | tf_op jit(solution)/shard_map/all_gather | solution.py:15
  245.0 10.5 %all-gather.1 = f32[4,1,4096]{2,1,0:T(1,128)S(1)} all-gather(f32[1,1,4096]{2,1,0:T(1,128)S(1)} %reshape.333), channel_id=1, replica_groups=mesh['seq'=64,'ctx'=4] {'ctx'}, dimensions={0}, use_global_device_ids=true | all-gather | bytes 81920 | tf_op jit(solution)/shard_map/all_gather | solution.py:15
  255.7 61.7 %all-gather.7.cloned.1.call-done = f32[4,4096,128]{2,1,0:T(8,128)} async-done(((f32[1,4096,128]{2,1,0:T(8,128)}), f32[4,4096,128]{2,1,0:T(8,128)}) %all-gather.7.cloned.1.call-update) | async-done | bytes 8388624 | tf_op jit(solution)/shard_map/all_gather | solution.py:15
  319.1 5.9 %slice.45 = f32[3,4096,128]{2,1,0:T(8,128)} slice(f32[4,4096,128]{2,1,0:T(8,128)} %all-gather.7.cloned.1.call-done), slice={[1:4], [0:4096], [0:128]} | slice | bytes 12582912 | tf_op jit(solution)/shard_map/slice | solution.py:17
  325.0 12.8 %while.29 = (s32[]{:T(128)}, f32[4096]{0:T(1024)S(1)}, f32[4096]{0:T(1024)S(1)}, f32[4096,128]{1,0:T(8,128)S(1)}, f32[3,4096]{1,0:T(4,128)S(1)}, /*index=5*/f32[...) while((s32[]{:T(128)}, f32[4096]{0:T(1024)S(1)}, f32[4096]{0:T(1024)S(1)}, f32[4096,128]{1,0:T(8,128)S(1)}, ...), condition=%wide.region_7.8_spmd, body=%wide.region_6.7_spmd.sunk | while | flops 1597442 | bytes 6520933 | solution.py:18
  325.0 4.2 %fusion.68 = f32[4096,128]{1,0:T(8,128)S(1)} fusion(f32[3,4096,128]{2,1,0:T(8,128)} %get-tuple-element.328, s32[]{:T(128)S(6)} %copy.108, f32[4096,128]{1,0:T(8,128)S(1)} %get-tuple-element.317, f32[4096]{0:T(1024)S(1)} %get-tuple-element.274, f32[4096]{0:T(1024)S(1)} %get-tuple-element.275), kind=kLoop, calls=%fused_computation.7.clone.1 | loop fusion | flops 1572864 | bytes 6324228 | tf_op jit(solution)/shard_map/while/body/eval_jaxpr/add | solution.py:50
  329.3 4.2 %fusion.68 = f32[4096,128]{1,0:T(8,128)S(1)} fusion(f32[3,4096,128]{2,1,0:T(8,128)} %get-tuple-element.328, s32[]{:T(128)S(6)} %copy.108, f32[4096,128]{1,0:T(8,128)S(1)} %get-tuple-element.317, f32[4096]{0:T(1024)S(1)} %get-tuple-element.274, f32[4096]{0:T(1024)S(1)} %get-tuple-element.275), kind=kLoop, calls=%fused_computation.7.clone.1 | loop fusion | flops 1572864 | bytes 6324228 | tf_op jit(solution)/shard_map/while/body/eval_jaxpr/add | solution.py:50
  333.6 4.2 %fusion.68 = f32[4096,128]{1,0:T(8,128)S(1)} fusion(f32[3,4096,128]{2,1,0:T(8,128)} %get-tuple-element.328, s32[]{:T(128)S(6)} %copy.108, f32[4096,128]{1,0:T(8,128)S(1)} %get-tuple-element.317, f32[4096]{0:T(1024)S(1)} %get-tuple-element.274, f32[4096]{0:T(1024)S(1)} %get-tuple-element.275), kind=kLoop, calls=%fused_computation.7.clone.1 | loop fusion | flops 1572864 | bytes 6324228 | tf_op jit(solution)/shard_map/while/body/eval_jaxpr/add | solution.py:50
  338.2 22.3 %all_to_all.70 = bf16[64,16,128]{2,1,0:T(8,128)(2,1)S(1)} all-to-all(bf16[64,16,128]{2,1,0:T(8,128)(2,1)S(1)} %fusion.31), channel_id=1, replica_groups=mesh['seq'=64,'ctx'=4] {'seq'}, dimensions={0} | all-to-all | bytes 524288 | tf_op jit(solution)/shard_map/all_to_all | solution.py:168
  (187 shorter events, 74.1 us)
Async XLA Ops:
  6.5 27.1 %copy-start.6 = (bf16[16,1024]{1,0:T(8,128)(2,1)S(1)}, bf16[16,1024]{1,0:T(8,128)(2,1)}, u32[]{:S(2)}) copy-start(bf16[16,1024]{1,0:T(8,128)(2,1)} %param.12) | copy-start | bytes 98308
  18.7 43.5 %all-to-all-start.2 = ((bf16[64,64,128]{2,0,1:T(8,128)(2,1)}), bf16[64,64,128]{2,0,1:T(8,128)(2,1)S(1)}, u32[]{:S(2)}, u32[]{:S(2)}) async-start(bf16[64,64,128]{2,0,1:T(8,128)(2,1)} %bitcast.36), calls=%async_computation.2 | async-start | bytes 2097152 | tf_op jit(solution)/shard_map/all_to_all | solution.py:110
  63.5 37.5 %all-to-all-start.1 = ((bf16[64,64,128]{2,0,1:T(8,128)(2,1)}), bf16[64,64,128]{2,0,1:T(8,128)(2,1)S(1)}, u32[]{:S(2)}, u32[]{:S(2)}) async-start(bf16[64,64,128]{2,0,1:T(8,128)(2,1)} %bitcast.20), calls=%async_computation.1 | async-start | bytes 2097152 | tf_op jit(solution)/shard_map/all_to_all | solution.py:103
  69.7 28.8 %all-gather.5.cloned.1.call-start = ((), (), s32[]{:S(2)}) async-start(), calls=%async_computation.4 | async-start | bytes 1310720 | tf_op jit(solution)/shard_map/all_gather | solution.py:67
  70.4 43.0 %copy-start.8 = (s32[1,64,1]{1,2,0:T(1,128)S(1)}, s32[1,64,1]{1,2,0:T(1,128)}, u32[]{:S(2)}) copy-start(s32[1,64,1]{1,2,0:T(1,128)} %param.17) | copy-start | bytes 772
  70.4 43.7 %copy-start.7 = (s32[1,64,1,12]{1,2,3,0:T(1,128)S(1)}, s32[1,64,1,12]{1,2,3,0:T(1,128)}, u32[]{:S(2)}) copy-start(s32[1,64,1,12]{1,2,3,0:T(1,128)} %param.16) | copy-start | bytes 9220
  100.9 16.5 %copy-start.3 = (bf16[64,64,128]{2,0,1:T(8,128)(2,1)}, bf16[64,64,128]{2,0,1:T(8,128)(2,1)S(1)}, u32[]{:S(2)}) copy-start(bf16[64,64,128]{2,0,1:T(8,128)(2,1)S(1)} %all-to-all-done.1) | copy-start | bytes 3145732
  100.9 40.2 %all-to-all-start = ((bf16[64,64,128]{2,0,1:T(8,128)(2,1)}), bf16[64,64,128]{2,0,1:T(8,128)(2,1)}, u32[]{:S(2)}, u32[]{:S(2)}) async-start(bf16[64,64,128]{2,0,1:T(8,128)(2,1)} %copy_bitcast_fusion), calls=%async_computation | async-start | bytes 2097152 | tf_op jit(solution)/shard_map/all_to_all | solution.py:71
  112.7 204.6 %all-gather.7.cloned.1.call-start = ((), (), s32[]{:S(2)}) async-start(), calls=%async_computation.5 | async-start | bytes 10485760 | tf_op jit(solution)/shard_map/all_gather | solution.py:15
  117.4 23.7 %copy-start.1 = (bf16[1,8192,128]{2,1,0:T(8,128)(2,1)S(1)}, bf16[1,8192,128]{2,1,0:T(8,128)(2,1)}, u32[]{:S(2)}) copy-start(bf16[1,8192,128]{2,1,0:T(8,128)(2,1)} %param.15) | copy-start | bytes 6291460
  146.8 2.4 copy-start
  150.7 1.6 copy-start.2
  158.0 2.4 copy-start
  161.9 1.6 copy-start.2
  169.2 2.4 copy-start
  173.1 1.6 copy-start.2
  180.3 2.4 copy-start
  184.2 1.6 copy-start.2
  191.5 2.4 copy-start
  195.4 1.6 copy-start.2
  202.7 2.4 copy-start
  206.6 1.6 copy-start.2
  213.8 2.4 copy-start
  217.8 1.6 copy-start.2
  225.0 2.4 copy-start
  228.9 1.6 copy-start.2
  230.5 3.1 copy-start.4
  230.6 3.1 copy-start.5
Sparse Core Ops, SparseCore 0:
  72.3 26.0 all-gather.4
  235.2 82.0 all-gather.6
where the time goes:
time: 369 us; the launch traced here: 368 us
  waiting for transfers between devices  128 us (35%)
  local copies, waits for them, and re-layouts  75 us (20%)
  blocking collectives  62.7 us (17%)
  matrix products  34.5 us (9%)
  starting transfers between devices  33 us (9%)
  other arithmetic  20.5 us (6%)
  between operations  13.7 us (4%)
    all_gather x1, waiting for transfers between devices, merged(): pieces = jax.tree.map(lambda part: lax.all_gather(part, axis), value)  61.7 us
    all_gather x1, waiting for transfers between devices, body(): lax.all_gather(queries, 'ctx', axis=0, tiled=True)  28 us
    all_to_all x1, blocking collectives, body(): lax.all_to_all(attended_rows, 'seq', split_axis=0, concat_axis=1, tiled=T...  22.3 us
    gather x8, local copies, waits for them, and re-layouts, cached_part(): tile_keys[listed_block].reshape(per_step, KQ * KROWS, head_size)  21.9 us
    gather x8, local copies, waits for them, and re-layouts, cached_part(): tile_values[listed_block].reshape(per_step, KQ * KROWS, head_size)  21.6 us
    all_gather x2, blocking collectives, merged(): pieces = jax.tree.map(lambda part: lax.all_gather(part, axis), value)  19.5 us
    all_to_all x1, waiting for transfers between devices, body(): lax.all_to_all(all_queries, 'seq', split_axis=1, concat_axis=0, tiled=True)  19.4 us
    dot_general x8, matrix products, cached_part(): jnp.einsum('pmt,pyt->pmy', query_group_block, selected_keys, preferred_el...  18.7 us
  transfers between devices with their start and end apart: 5, of which 4 were waited for; matrix products, arithmetic and copies ran while one was open for 3% of the time, Pallas kernels for 0%

commit v1 on v0

v1 whole, which is shorter than its diff:
```python
import math

import jax
import jax.numpy as jnp
from jax import lax
from jax.experimental import pallas as pl
from jax.experimental.pallas import tpu as pltpu
from jax.sharding import PartitionSpec as P

HEADS = 8
ROWS = 64
KROWS = 128
KQ = 12
D = 128
NB = 8
CTX = 4
ZS = 8
PIECE = ROWS // CTX
WIDE = HEADS * D
MSG = WIDE + D
LAG = 2
C = math.log2(math.e) / math.sqrt(D)
NT = (((1,), (1,)), ((), ()))
MESH = pl.DeviceIdType.MESH
F32, BF16 = jnp.float32, jnp.bfloat16


def member(z, group):
    near_z = jnp.minimum(z, ZS - 1 - z)
    return 2 * jnp.where(group % 2 == 0, near_z, 3 - near_z) + jnp.where(z >= 4, 1, 0)


def z_of(e, group):
    near_z = jnp.where(group % 2 == 0, e // 2, 3 - e // 2)
    return jnp.where(e % 2 == 0, near_z, ZS - 1 - near_z)


def kernel(
    q_hbm, nk_hbm, nv_hbm, k_hbm, v_hbm, tbl_hbm, out_hbm,
    q_buf, k_buf, v_buf, nks, nvs, kvs, kvn, tbl_buf, tbl, s_buf, acc, lse, nacc, nlse, msg, rcv, fin,
    load_sem, q_send, q_recv, y_send, y_recv, kv_send, kv_recv, t_send, t_recv, m_send, m_recv, f_send, f_recv, smem_sem,
):
    s, c = lax.axis_index("seq"), lax.axis_index("ctx")
    x, z, core = s // 16, (s // 2) % ZS, s % 2
    group, e = s // HEADS, s % HEADS
    zt = z_of(e, group)
    mine = x * 2 + core

    loads = [
        pltpu.make_async_copy(nk_hbm, nks, load_sem.at[0]),
        pltpu.make_async_copy(nv_hbm, nvs, load_sem.at[1]),
        pltpu.make_async_copy(k_hbm, k_buf, load_sem.at[2]),
        pltpu.make_async_copy(v_hbm, v_buf, load_sem.at[3]),
    ]
    for load in loads:
        load.start()

    def signal(seq, ctx):
        pl.semaphore_signal(barrier, inc=1, device_id=(seq, ctx), device_id_type=MESH)

    barrier = pltpu.get_barrier_semaphore()
    expected = jnp.int32(7 + 3)
    for j in range(1, CTX):
        signal(s, (c + j) % CTX)
    for j in range(1, HEADS):
        signal(group * HEADS + (e + j) % HEADS, c)
    for n in range(NB):
        seq = ((n // 2) * ZS + zt) * 2 + n % 2
        pl.when(seq != s)(lambda seq=seq: signal(seq, c))
    near_b = c * ZS + zt
    for role in range(2):
        for i in range(8):
            seq, ctx = (near_b - role) * 2 + i % 2, i // 2
            ok = (near_b - role >= 0) & ((seq != s) | (ctx != c))
            pl.when(ok)(lambda seq=seq, ctx=ctx: signal(seq, ctx))

    def q_dest(g):
        return g * HEADS + member(z, g)

    def kv_dest(role, g):
        b = x * ZS + z + role
        return g * HEADS + member(b % ZS, g), b // ZS

    for g in range(8):
        expected += jnp.where(q_dest(g) != s, 1, 0)
        for role in range(2):
            seq, ctx = kv_dest(role, g)
            expected += jnp.where((ctx < CTX) & ((seq != s) | (ctx != c)), 1, 0)

    loads[0].wait()
    loads[1].wait()
    for g in range(8):
        kvs[g, :, :D] = nks[:, g * D:(g + 1) * D]
        kvs[g, :, D:] = nvs[:, g * D:(g + 1) * D]

    @pl.when(near_b == 0)
    def _():
        kvn[:KROWS] = jnp.zeros((KROWS, 2 * D), BF16)

    pl.semaphore_wait(barrier, expected)

    def remote(src, dst, send, recv, seq, ctx):
        return pltpu.make_async_remote_copy(
            src_ref=src, dst_ref=dst, send_sem=send, recv_sem=recv, device_id=(seq, ctx), device_id_type=MESH
        )

    def t_copy(j):
        to = (e + j) % HEADS
        return remote(
            tbl_hbm.at[z_of(to, group)], tbl_buf.at[e], t_send.at[j], t_recv, group * HEADS + to, c
        )

    t_own = pltpu.make_async_copy(tbl_hbm.at[zt], tbl_buf.at[e], t_recv)
    t_own.start()
    for j in range(1, HEADS):
        t_copy(j).start()

    rows_c = pl.ds(pl.multiple_of(c * PIECE, PIECE), PIECE)

    def q_copy(g):
        src, dst = q_hbm.at[:, pl.ds(g * WIDE, WIDE)], q_buf.at[mine, rows_c]
        return (
            remote(src, dst, q_send.at[g], q_recv.at[mine], q_dest(g), c),
            pltpu.make_async_copy(src, dst, q_recv.at[mine]),
        )

    def start_either(copies, own):
        pl.when(own)(copies[1].start)
        pl.when(jnp.logical_not(own))(copies[0].start)

    for g in range(8):
        start_either(q_copy(g), q_dest(g) == s)

    def kv_copy(role, g):
        seq, ctx = kv_dest(role, g)
        row = (1 - role) * KROWS + core * ROWS + c * PIECE
        dst = kvn.at[pl.ds(pl.multiple_of(row, PIECE), PIECE)]
        own = (seq == s) & (ctx == c)
        return (
            remote(kvs.at[g], dst, kv_send.at[role * 8 + g], kv_recv, seq, ctx),
            pltpu.make_async_copy(kvs.at[g], dst, kv_recv),
            own,
            (ctx < CTX) & jnp.logical_not(own),
        )

    for role in range(2):
        for g in range(8):
            there, here, own, other = kv_copy(role, g)
            pl.when(own)(here.start)
            pl.when(other)(there.start)

    def landed(ref, sem):
        pltpu.make_async_copy(ref, ref, sem).wait()

    def y_copy(n, j):
        piece = q_buf.at[n, rows_c]
        return remote(piece, piece, y_send.at[j - 1, n], y_recv.at[j - 1, n], s, (c + j) % CTX)

    def forward(n, _):
        landed(q_buf.at[n, rows_c], q_recv.at[n])
        for j in range(1, CTX):
            y_copy(n, j).start()
        return 0

    lax.fori_loop(0, NB, forward, 0)

    landed(tbl_buf, t_recv)
    to_smem = pltpu.make_async_copy(tbl_buf, tbl, smem_sem)
    to_smem.start()
    loads[2].wait()
    loads[3].wait()
    to_smem.wait()

    lane = lax.broadcasted_iota(jnp.int32, (1, D), 1)

    def finish(o, l, m, h, o_ref, total):
        o_ref[:, h * D:(h + 1) * D] = o * (1.0 / l)
        return jnp.where(lane % HEADS == h, m + jnp.log2(l), total)

    def near(n):
        @pl.when(n % 2 == 0)
        def _():
            pl.when(near_b > 0)(lambda: landed(kvn, kv_recv))
            pl.when(near_b == 0)(lambda: landed(kvn.at[pl.ds(KROWS, KROWS)], kv_recv))

        key = lax.broadcasted_iota(jnp.int32, (ROWS, 2 * KROWS), 1)
        row = lax.broadcasted_iota(jnp.int32, (ROWS, 2 * KROWS), 0)
        first = jnp.where(near_b > 0, 0, KROWS)
        visible = (key >= first) & (key <= row + (KROWS + (n % 2) * ROWS))
        total = jnp.zeros((ROWS, D), F32)
        for h in range(HEADS):
            sc = lax.dot_general(q_buf[n, :, h * D:(h + 1) * D], kvn[:, :D], NT, preferred_element_type=F32)
            sc = jnp.where(visible, sc * C, -jnp.inf)
            m = jnp.max(sc, axis=1, keepdims=True)
            p = jnp.exp2(sc - m)
            l = jnp.sum(p, axis=1, keepdims=True)
            o = jnp.dot(p.astype(BF16), kvn[:, D:], preferred_element_type=F32)
            total = finish(o, l, m, h, nacc, total)
        nlse[...] = total

    def attend(n):
        tops = []
        for h in range(HEADS):
            qq = q_buf[n, :, h * D:(h + 1) * D]
            m = jnp.full((ROWS, KROWS), -jnp.inf, F32)
            for t in range(0, KQ, 2):
                kk = jnp.concatenate([k_buf[tbl[h, n, t + i]] for i in range(2)], 0)
                sc = lax.dot_general(qq, kk, NT, preferred_element_type=F32)
                s_buf[h, :, t * KROWS:(t + 2) * KROWS] = sc
                m = jnp.maximum(m, jnp.maximum(sc[:, :KROWS], sc[:, KROWS:]))
            tops.append(jnp.max(m, axis=1, keepdims=True) * C)
        total = jnp.zeros((ROWS, D), F32)
        for h in range(HEADS):
            used, m = tbl[h, n, KQ], tops[h]
            o = jnp.zeros((ROWS, D), F32)
            l = jnp.zeros((ROWS, KROWS), F32)
            for t in range(0, KQ, 2):
                parts = []
                for i in range(2):
                    shift = m + jnp.where(t + i < used, 0.0, jnp.inf)
                    p = jnp.exp2(s_buf[h, :, (t + i) * KROWS:(t + i + 1) * KROWS] * C - shift)
                    l = l + p
                    parts.append(p.astype(BF16))
                vv = jnp.concatenate([v_buf[tbl[h, n, t + i]] for i in range(2)], 0)
                o = o + jnp.dot(jnp.concatenate(parts, 1), vv, preferred_element_type=F32)
            total = finish(o, jnp.sum(l, axis=1, keepdims=True), m, h, acc, total)
        lse[...] = total

    def merge_near():
        top = jnp.maximum(lse[...], nlse[...])
        w0, w1 = jnp.exp2(lse[...] - top), jnp.exp2(nlse[...] - top)
        both = w0 + w1
        w0, w1 = w0 / both, w1 / both
        for h in range(HEADS):
            cols = slice(h * D, (h + 1) * D)
            acc[:, cols] = acc[:, cols] * w0[:, h:h + 1] + nacc[:, cols] * w1[:, h:h + 1]
        lse[...] = top + jnp.log2(both)

    def pack(n):
        for h in range(HEADS):
            msg[n, :, h * D:(h + 1) * D] = acc[:, h * D:(h + 1) * D].astype(BF16)
        full = lse[...]
        one = full.astype(BF16)
        rest = full - one.astype(F32)
        two = rest.astype(BF16)
        three = (rest - two.astype(F32)).astype(BF16)
        terms = jnp.where(lane < HEADS, one.astype(F32), jnp.where(lane < 2 * HEADS, two.astype(F32), three.astype(F32)))
        msg[n, :, WIDE:] = terms.astype(BF16)

    def m_copy(n, j):
        to = (c + j) % CTX
        src = msg.at[n, pl.ds(pl.multiple_of(to * PIECE, PIECE), PIECE)]
        return remote(src, rcv.at[j - 1, n], m_send.at[j - 1, n], m_recv.at[j - 1, n], s, to)

    def f_seq(n):
        return ((n // 2) * ZS + zt) * 2 + n % 2

    def f_copy(n):
        dst = out_hbm.at[:, pl.ds(pl.multiple_of(group * WIDE, WIDE), WIDE)]
        return (
            remote(fin.at[n], dst, f_send.at[n], f_recv, f_seq(n), c),
            pltpu.make_async_copy(fin.at[n], dst, f_recv),
        )

    def join(n):
        for j in range(1, CTX):
            landed(rcv.at[j - 1, n], m_recv.at[j - 1, n])
        parts = [msg.at[n, rows_c]] + [rcv.at[j, n] for j in range(CTX - 1)]
        logs = []
        for part in parts:
            terms = part[:, WIDE:].astype(F32)
            logs.append(terms + pltpu.roll(terms, D - HEADS, 1) + pltpu.roll(terms, D - 2 * HEADS, 1))
        top = jnp.maximum(jnp.maximum(logs[0], logs[1]), jnp.maximum(logs[2], logs[3]))
        weights = [jnp.exp2(log - top) for log in logs]
        inverse = 1.0 / (weights[0] + weights[1] + weights[2] + weights[3])
        weights = [w * inverse for w in weights]
        for h in range(HEADS):
            cols = slice(h * D, (h + 1) * D)
            o = sum(part[:, cols].astype(F32) * w[:, h:h + 1] for part, w in zip(parts, weights))
            fin[n, :, cols] = o.astype(BF16)
        start_either(f_copy(n), f_seq(n) == s)

    def step(n, _):
        @pl.when(n < NB)
        def _():
            for j in range(1, CTX):
                rows = pl.ds(pl.multiple_of(((c + CTX - j) % CTX) * PIECE, PIECE), PIECE)
                landed(q_buf.at[n, rows], y_recv.at[j - 1, n])
            is_near = n // 2 == c
            pl.when(is_near)(lambda: near(n))
            attend(n)
            pl.when(is_near)(merge_near)
            pack(n)
            for j in range(1, CTX):
                m_copy(n, j).start()

        pl.when(n >= LAG)(lambda: join(n - LAG))
        return 0

    lax.fori_loop(0, NB + LAG, step, 0)

    for j in range(1, HEADS):
        t_copy(j).wait_send()
    for g in range(8):
        pl.when(q_dest(g) != s)(q_copy(g)[0].wait_send)
        for role in range(2):
            there, _, _, other = kv_copy(role, g)
            pl.when(other)(there.wait_send)

    def drain(n, _):
        for j in range(1, CTX):
            y_copy(n, j).wait_send()
            m_copy(n, j).wait_send()
        pl.when(f_seq(n) != s)(f_copy(n)[0].wait_send)
        return 0

    lax.fori_loop(0, NB, drain, 0)
    landed(out_hbm, f_recv)


def body(queries, new_token_keys, new_token_values, cache_keys, cache_values, block_ids, block_counts):
    used = block_counts[0, :, :]
    slot = jnp.arange(KQ, dtype=jnp.int32)[None, :]
    ids = block_ids[0, :, 0, :]
    ids = jnp.where(slot < used, ids, ids[:, :1])
    table = jnp.concatenate([ids, used, jnp.zeros((ids.shape[0], D - KQ - 1), jnp.int32)], axis=1)
    table = table.reshape(CTX, ZS, 2, D).transpose(1, 0, 2, 3).reshape(ZS, NB, D)
    blocks = cache_keys.shape[1] // KROWS
    hbm = pl.BlockSpec(memory_space=pl.ANY)
    dma = pltpu.SemaphoreType.DMA
    return pl.pallas_call(
        kernel,
        out_shape=jax.ShapeDtypeStruct(queries.shape, BF16),
        in_specs=[hbm] * 6,
        out_specs=hbm,
        scratch_shapes=[
            pltpu.VMEM((NB, ROWS, WIDE), BF16),
            pltpu.VMEM((blocks, KROWS, D), BF16),
            pltpu.VMEM((blocks, KROWS, D), BF16),
            pltpu.VMEM((PIECE, WIDE), BF16),
            pltpu.VMEM((PIECE, WIDE), BF16),
            pltpu.VMEM((8, PIECE, 2 * D), BF16),
            pltpu.VMEM((2 * KROWS, 2 * D), BF16),
            pltpu.VMEM((HEADS, NB, D), jnp.int32),
            pltpu.SMEM((HEADS, NB, D), jnp.int32),
            pltpu.VMEM((HEADS, ROWS, KQ * KROWS), F32),
            pltpu.VMEM((ROWS, WIDE), F32),
            pltpu.VMEM((ROWS, D), F32),
            pltpu.VMEM((ROWS, WIDE), F32),
            pltpu.VMEM((ROWS, D), F32),
            pltpu.VMEM((NB, ROWS, MSG), BF16),
            pltpu.VMEM((CTX - 1, NB, PIECE, MSG), BF16),
            pltpu.VMEM((NB, PIECE, WIDE), BF16),
            dma((4,)), dma((8,)), dma((NB,)), dma((CTX - 1, NB)), dma((CTX - 1, NB)), dma((16,)), dma, dma((HEADS,)), dma,
            dma((CTX - 1, NB)), dma((CTX - 1, NB)), dma((NB,)), dma, dma,
        ],
        compiler_params=pltpu.CompilerParams(
            collective_id=0, has_side_effects=True, vmem_limit_bytes=48 << 20
        ),
        name="attend_all",
    )(
        queries, new_token_keys, new_token_values,
        cache_keys.reshape(blocks, KROWS, D), cache_values.reshape(blocks, KROWS, D), table,
    )


def solution(mesh):
    return jax.shard_map(
        body,
        mesh=mesh,
        in_specs=(
            P(("seq", "ctx"), None),
            P(("seq", "ctx"), None),
            P(("seq", "ctx"), None),
            P("seq", "ctx", None),
            P("seq", "ctx", None),
            P("seq", None, "ctx", None),
            P("seq", None, "ctx"),
        ),
        out_specs=P(("seq", "ctx"), None),
        check_vma=False,
    )
```

time: 369 us -> 72.6 us (0.20)
  the two profiles are of different devices: /device:TPU:1 before, /device:TPU:7 now
where the time goes in v1:
time: 72.6 us; the launch traced here: 72.2 us
  Pallas kernels  61 us (84%)
  local copies, waits for them, and re-layouts  9.69 us (13%)
  other arithmetic  1.49 us (2%)
    pallas_call x1, Pallas kernels, body(): pl.pallas_call(kernel, out_shape=jax.ShapeDtypeStruct(queries.shape, BF16...  61 us
    unnamed x14, local copies, waits for them, and re-layouts  8.33 us

profile of v1, /device:TPU:7, one launch (start us, length us, event | category | flops | bytes accessed | tf_op | source)
XLA Modules:
  0.0 72.2 jit_solution(3050861133934637573)
XLA Ops:
  0.0 0.5 broadcast.18
  0.5 1.3 %reduce.9 = s32[64]{0:T(128)S(1)} reduce(s32[1,64,1]{1,2,0:T(1,128)} %param.13, s32[]{:T(128)} %broadcast.18), dimensions={0,2}, to_apply=%param.13.reduce_sub_computation.5 | reduce | bytes 516 | tf_op args[6]
  1.8 0.1 pad.2.clone
  1.9 0.7 copy.19
  2.6 0.1 broadcast_in_dim.14
  2.7 0.1 lt.17
  2.8 0.8 %concatenate.6 = s32[4,8,2,1]{2,1,0,3:T(8,128)S(1)} reshape(s32[64]{0:T(128)} %bitcast.16) | data formatting | bytes 512 | tf_op jit(solution)/shard_map/concatenate | solution.py:326
  3.6 0.3 copy.14
  3.9 0.8 %copy.12 = s32[1,64,1,12]{3,1,2,0:T(8,128)S(1)} copy(s32[1,64,1,12]{1,2,3,0:T(1,128)} %param.12) | data formatting | bytes 6144 | tf_op args[5]
  4.7 0.2 add_add_fusion
  4.9 0.0 copy-start
  4.9 1.6 %copy-done = bf16[1,8192,128]{2,1,0:T(8,128)(2,1)S(1)} copy-done((bf16[1,8192,128]{2,1,0:T(8,128)(2,1)S(1)}, bf16[1,8192,128]{2,1,0:T(8,128)(2,1)}, u32[]{:S(2)}) %copy-start) | copy-done | bytes 2097176
  6.5 0.0 copy-start.1
  6.5 1.6 %copy-done.1 = bf16[1,8192,128]{2,1,0:T(8,128)(2,1)S(1)} copy-done((bf16[1,8192,128]{2,1,0:T(8,128)(2,1)S(1)}, bf16[1,8192,128]{2,1,0:T(8,128)(2,1)}, u32[]{:S(2)}) %copy-start.1) | copy-done | bytes 2097176
  8.1 0.0 copy-start.2
  8.1 0.9 %copy-done.2 = bf16[16,8192]{1,0:T(8,128)(2,1)S(1)} copy-done((bf16[16,8192]{1,0:T(8,128)(2,1)S(1)}, bf16[16,8192]{1,0:T(8,128)(2,1)}, u32[]{:S(2)}) %copy-start.2) | copy-done | bytes 262168
  9.0 0.0 copy-start.3
  9.0 0.8 %copy-done.3 = bf16[16,1024]{1,0:T(8,128)(2,1)S(1)} copy-done((bf16[16,1024]{1,0:T(8,128)(2,1)S(1)}, bf16[16,1024]{1,0:T(8,128)(2,1)}, u32[]{:S(2)}) %copy-start.3) | copy-done | bytes 32792
  9.8 0.0 copy-start.4
  9.8 0.8 %copy-done.4 = bf16[16,1024]{1,0:T(8,128)(2,1)S(1)} copy-done((bf16[16,1024]{1,0:T(8,128)(2,1)S(1)}, bf16[16,1024]{1,0:T(8,128)(2,1)}, u32[]{:S(2)}) %copy-start.4) | copy-done | bytes 32792
  10.5 61.0 %attend_all.1 = bf16[16,8192]{1,0:T(8,128)(2,1)S(1)} custom-call(bf16[16,8192]{1,0:T(8,128)(2,1)S(1)} %copy-done.2, bf16[16,1024]{1,0:T(8,128)(2,1)S(1)} %copy-done.3, bf16[16,1024]{1,0:T(8,128)(2,1)S(1)} %copy-done.4, bf16[64,128,128]{2,1,0:T(8,128)(2,1)S(1)} %bitcast.11, bf16[64,128,128]{2,1,0:T(8,128)(2,1)S(1)} %bitcast.12, s32[8,8,128]{2,1,0:T(8,128)S(1)} %bitcast.13), custom_call_target="tpu_custom_call" | custom-call | tf_op jit(solution)/shard_map/attend_all/pallas_call | solution.py:331
  71.5 0.7 copy.21
  (2 shorter events, 0.0 us)
Async XLA Ops:
  4.9 1.6 %copy-start = (bf16[1,8192,128]{2,1,0:T(8,128)(2,1)S(1)}, bf16[1,8192,128]{2,1,0:T(8,128)(2,1)}, u32[]{:S(2)}) copy-start(bf16[1,8192,128]{2,1,0:T(8,128)(2,1)} %param.10) | copy-start | bytes 6291460
  6.5 1.6 %copy-start.1 = (bf16[1,8192,128]{2,1,0:T(8,128)(2,1)S(1)}, bf16[1,8192,128]{2,1,0:T(8,128)(2,1)}, u32[]{:S(2)}) copy-start(bf16[1,8192,128]{2,1,0:T(8,128)(2,1)} %param.11) | copy-start | bytes 6291460
  8.1 0.9 %copy-start.2 = (bf16[16,8192]{1,0:T(8,128)(2,1)S(1)}, bf16[16,8192]{1,0:T(8,128)(2,1)}, u32[]{:S(2)}) copy-start(bf16[16,8192]{1,0:T(8,128)(2,1)} %q_hbm.1) | copy-start | bytes 786436
  9.0 0.8 %copy-start.3 = (bf16[16,1024]{1,0:T(8,128)(2,1)S(1)}, bf16[16,1024]{1,0:T(8,128)(2,1)}, u32[]{:S(2)}) copy-start(bf16[16,1024]{1,0:T(8,128)(2,1)} %nk_hbm.1) | copy-start | bytes 98308
  9.8 0.8 %copy-start.4 = (bf16[16,1024]{1,0:T(8,128)(2,1)S(1)}, bf16[16,1024]{1,0:T(8,128)(2,1)}, u32[]{:S(2)}) copy-start(bf16[16,1024]{1,0:T(8,128)(2,1)} %nv_hbm.1) | copy-start | bytes 98308

commit v2 on v1

--- a/solution.py
+++ b/solution.py
@@ -13,6 +13,7 @@
 KQ = 12
 D = 128
 NB = 8
+BLOCKS = 64
 CTX = 4
 ZS = 8
 PIECE = ROWS // CTX
@@ -36,8 +37,8 @@
 
 
 def kernel(
-    q_hbm, nk_hbm, nv_hbm, k_hbm, v_hbm, tbl_hbm, out_hbm,
-    q_buf, k_buf, v_buf, nks, nvs, kvs, kvn, tbl_buf, tbl, s_buf, acc, lse, nacc, nlse, msg, rcv, fin,
+    q_hbm, nk_hbm, nv_hbm, k_hbm, v_hbm, ids_hbm, used_hbm, out_hbm,
+    q_buf, k_buf, v_buf, nks, nvs, kvs, kvn, ids, used, own_tbl, tbl_buf, tbl, s_buf, acc, lse, nacc, nlse, msg, rcv, fin,
     load_sem, q_send, q_recv, y_send, y_recv, kv_send, kv_recv, t_send, t_recv, m_send, m_recv, f_send, f_recv, smem_sem,
 ):
     s, c = lax.axis_index("seq"), lax.axis_index("ctx")
@@ -46,11 +47,16 @@
     zt = z_of(e, group)
     mine = x * 2 + core
 
+    def f_seq(n):
+        return ((n // 2) * ZS + zt) * 2 + n % 2
+
     loads = [
         pltpu.make_async_copy(nk_hbm, nks, load_sem.at[0]),
         pltpu.make_async_copy(nv_hbm, nvs, load_sem.at[1]),
         pltpu.make_async_copy(k_hbm, k_buf, load_sem.at[2]),
         pltpu.make_async_copy(v_hbm, v_buf, load_sem.at[3]),
+        pltpu.make_async_copy(ids_hbm, ids, load_sem.at[4]),
+        pltpu.make_async_copy(used_hbm, used, load_sem.at[5]),
     ]
     for load in loads:
         load.start()
@@ -87,8 +93,12 @@
             seq, ctx = kv_dest(role, g)
             expected += jnp.where((ctx < CTX) & ((seq != s) | (ctx != c)), 1, 0)
 
-    loads[0].wait()
-    loads[1].wait()
+    for i in (0, 1, 4, 5):
+        loads[i].wait()
+    own_tbl[...] = jnp.zeros_like(own_tbl)
+    for t in range(KQ):
+        own_tbl[t:t + 1, :BLOCKS] = jnp.where(t < used[0], ids[t], ids[0])
+    own_tbl[KQ:KQ + 1, :BLOCKS] = used[0]
     for g in range(8):
         kvs[g, :, :D] = nks[:, g * D:(g + 1) * D]
         kvs[g, :, D:] = nvs[:, g * D:(g + 1) * D]
@@ -106,11 +116,9 @@
 
     def t_copy(j):
         to = (e + j) % HEADS
-        return remote(
-            tbl_hbm.at[z_of(to, group)], tbl_buf.at[e], t_send.at[j], t_recv, group * HEADS + to, c
-        )
-
-    t_own = pltpu.make_async_copy(tbl_hbm.at[zt], tbl_buf.at[e], t_recv)
+        return remote(own_tbl, tbl_buf.at[e], t_send.at[j], t_recv, group * HEADS + to, c)
+
+    t_own = pltpu.make_async_copy(own_tbl, tbl_buf.at[e], t_recv)
     t_own.start()
     for j in range(1, HEADS):
         t_copy(j).start()
@@ -199,29 +207,30 @@
         nlse[...] = total
 
     def attend(n):
+        block = f_seq(n)
         tops = []
         for h in range(HEADS):
             qq = q_buf[n, :, h * D:(h + 1) * D]
             m = jnp.full((ROWS, KROWS), -jnp.inf, F32)
             for t in range(0, KQ, 2):
-                kk = jnp.concatenate([k_buf[tbl[h, n, t + i]] for i in range(2)], 0)
+                kk = jnp.concatenate([k_buf[tbl[h, t + i, block]] for i in range(2)], 0)
                 sc = lax.dot_general(qq, kk, NT, preferred_element_type=F32)
                 s_buf[h, :, t * KROWS:(t + 2) * KROWS] = sc
                 m = jnp.maximum(m, jnp.maximum(sc[:, :KROWS], sc[:, KROWS:]))
             tops.append(jnp.max(m, axis=1, keepdims=True) * C)
         total = jnp.zeros((ROWS, D), F32)
         for h in range(HEADS):
-            used, m = tbl[h, n, KQ], tops[h]
+            count, m = tbl[h, KQ, block], tops[h]
             o = jnp.zeros((ROWS, D), F32)
             l = jnp.zeros((ROWS, KROWS), F32)
             for t in range(0, KQ, 2):
                 parts = []
                 for i in range(2):
-                    shift = m + jnp.where(t + i < used, 0.0, jnp.inf)
+                    shift = m + jnp.where(t + i < count, 0.0, jnp.inf)
                     p = jnp.exp2(s_buf[h, :, (t + i) * KROWS:(t + i + 1) * KROWS] * C - shift)
                     l = l + p
                     parts.append(p.astype(BF16))
-                vv = jnp.concatenate([v_buf[tbl[h, n, t + i]] for i in range(2)], 0)
+                vv = jnp.concatenate([v_buf[tbl[h, t + i, block]] for i in range(2)], 0)
                 o = o + jnp.dot(jnp.concatenate(parts, 1), vv, preferred_element_type=F32)
             total = finish(o, jnp.sum(l, axis=1, keepdims=True), m, h, acc, total)
         lse[...] = total
@@ -251,9 +260,6 @@
         to = (c + j) % CTX
         src = msg.at[n, pl.ds(pl.multiple_of(to * PIECE, PIECE), PIECE)]
         return remote(src, rcv.at[j - 1, n], m_send.at[j - 1, n], m_recv.at[j - 1, n], s, to)
-
-    def f_seq(n):
-        return ((n // 2) * ZS + zt) * 2 + n % 2
 
     def f_copy(n):
         dst = out_hbm.at[:, pl.ds(pl.multiple_of(group * WIDE, WIDE), WIDE)]
@@ -319,19 +325,15 @@
 
 
 def body(queries, new_token_keys, new_token_values, cache_keys, cache_values, block_ids, block_counts):
-    used = block_counts[0, :, :]
-    slot = jnp.arange(KQ, dtype=jnp.int32)[None, :]
-    ids = block_ids[0, :, 0, :]
-    ids = jnp.where(slot < used, ids, ids[:, :1])
-    table = jnp.concatenate([ids, used, jnp.zeros((ids.shape[0], D - KQ - 1), jnp.int32)], axis=1)
-    table = table.reshape(CTX, ZS, 2, D).transpose(1, 0, 2, 3).reshape(ZS, NB, D)
+    ids = block_ids[0].transpose(2, 1, 0)
+    used = block_counts.transpose(0, 2, 1)
     blocks = cache_keys.shape[1] // KROWS
     hbm = pl.BlockSpec(memory_space=pl.ANY)
     dma = pltpu.SemaphoreType.DMA
     return pl.pallas_call(
         kernel,
         out_shape=jax.ShapeDtypeStruct(queries.shape, BF16),
-        in_specs=[hbm] * 6,
+        in_specs=[hbm] * 7,
         out_specs=hbm,
         scratch_shapes=[
             pltpu.VMEM((NB, ROWS, WIDE), BF16),
@@ -341,8 +343,11 @@
             pltpu.VMEM((PIECE, WIDE), BF16),
             pltpu.VMEM((8, PIECE, 2 * D), BF16),
             pltpu.VMEM((2 * KROWS, 2 * D), BF16),
-            pltpu.VMEM((HEADS, NB, D), jnp.int32),
-            pltpu.SMEM((HEADS, NB, D), jnp.int32),
+            pltpu.VMEM(ids.shape, jnp.int32),
+            pltpu.VMEM(used.shape, jnp.int32),
+            pltpu.VMEM((16, D), jnp.int32),
+            pltpu.VMEM((HEADS, 16, D), jnp.int32),
+            pltpu.SMEM((HEADS, 16, D), jnp.int32),
             pltpu.VMEM((HEADS, ROWS, KQ * KROWS), F32),
             pltpu.VMEM((ROWS, WIDE), F32),
             pltpu.VMEM((ROWS, D), F32),
@@ -351,16 +356,16 @@
             pltpu.VMEM((NB, ROWS, MSG), BF16),
             pltpu.VMEM((CTX - 1, NB, PIECE, MSG), BF16),
             pltpu.VMEM((NB, PIECE, WIDE), BF16),
-            dma((4,)), dma((8,)), dma((NB,)), dma((CTX - 1, NB)), dma((CTX - 1, NB)), dma((16,)), dma, dma((HEADS,)), dma,
+            dma((6,)), dma((8,)), dma((NB,)), dma((CTX - 1, NB)), dma((CTX - 1, NB)), dma((16,)), dma, dma((HEADS,)), dma,
             dma((CTX - 1, NB)), dma((CTX - 1, NB)), dma((NB,)), dma, dma,
         ],
         compiler_params=pltpu.CompilerParams(
-            collective_id=0, has_side_effects=True, vmem_limit_bytes=48 << 20
+            collective_id=0, has_side_effects=True
         ),
         name="attend_all",
     )(
         queries, new_token_keys, new_token_values,
-        cache_keys.reshape(blocks, KROWS, D), cache_values.reshape(blocks, KROWS, D), table,
+        cache_keys.reshape(blocks, KROWS, D), cache_values.reshape(blocks, KROWS, D), ids, used,
     )
 
 

time: 72.6 us -> 62.5 us (0.86)
  local copies, waits for them, and re-layouts: 9.69 us -> 1.67 us
  other arithmetic: 1.49 us -> 0 us
    unnamed x14 -> x1, local copies, waits for them, and re-layouts: 8.33 us -> 1.67 us
    unnamed x1 -> x0, other arithmetic: 1.32 us -> none
    concatenate x3 -> x0, local copies, waits for them, and re-layouts: 1.14 us -> none  [body(): jnp.concatenate([ids, used, jnp.zeros((ids.shape[0], D - KQ - 1), jnp.int...]
where the time goes in v2:
time: 62.5 us; the launch traced here: 62.3 us
  Pallas kernels  60.6 us (97%)
  local copies, waits for them, and re-layouts  1.67 us (3%)
    pallas_call x1, Pallas kernels, body(): pl.pallas_call(kernel, out_shape=jax.ShapeDtypeStruct(queries.shape, BF16...  60.6 us
    unnamed x1, local copies, waits for them, and re-layouts  1.67 us

profile of v2, /device:TPU:7, one launch (start us, length us, event | category | flops | bytes accessed | tf_op | source)
XLA Modules:
  0.0 62.3 jit_solution(9038977042040636398)
XLA Ops:
  0.0 60.6 %attend_all.1 = bf16[16,8192]{1,0:T(8,128)(2,1)} custom-call(bf16[16,8192]{1,0:T(8,128)(2,1)} %q_hbm.1, bf16[16,1024]{1,0:T(8,128)(2,1)} %nk_hbm.1, bf16[16,1024]{1,0:T(8,128)(2,1)} %nv_hbm.1, bf16[64,128,128]{2,1,0:T(8,128)(2,1)} %bitcast.6, bf16[64,128,128]{2,1,0:T(8,128)(2,1)} %bitcast.7, s32[12,1,64]{2,1,0:T(1,128)} %bitcast.8, s32[1,1,64]{2,1,0:T(1,128)} %bitcast.9), custom_call_target="tpu_custom_call" | custom-call | tf_op jit(solution)/shard_map/attend_all/pallas_call | solution.py:333
  60.7 1.7 %copy.9 = bf16[16,8192]{1,0:T(8,128)(2,1)} copy(bf16[16,8192]{1,0:T(8,128)(2,1)} %attend_all.1) | data formatting | bytes 524288

commit v3 on v2

--- a/solution.py
+++ b/solution.py
@@ -19,7 +19,8 @@
 PIECE = ROWS // CTX
 WIDE = HEADS * D
 MSG = WIDE + D
-LAG = 2
+LAG = 4
+AHEAD = 3
 C = math.log2(math.e) / math.sqrt(D)
 NT = (((1,), (1,)), ((), ()))
 MESH = pl.DeviceIdType.MESH
@@ -125,19 +126,24 @@
 
     rows_c = pl.ds(pl.multiple_of(c * PIECE, PIECE), PIECE)
 
-    def q_copy(g):
-        src, dst = q_hbm.at[:, pl.ds(g * WIDE, WIDE)], q_buf.at[mine, rows_c]
+    def order(u):
+        return (group + u) % NB
+
+    def q_copy(t):
+        g = (mine + NB - t) % NB
+        src, dst = q_hbm.at[:, pl.ds(pl.multiple_of(g * WIDE, WIDE), WIDE)], q_buf.at[mine, rows_c]
         return (
-            remote(src, dst, q_send.at[g], q_recv.at[mine], q_dest(g), c),
+            remote(src, dst, q_send.at[t], q_recv.at[mine], q_dest(g), c),
             pltpu.make_async_copy(src, dst, q_recv.at[mine]),
+            q_dest(g) == s,
         )
 
-    def start_either(copies, own):
-        pl.when(own)(copies[1].start)
-        pl.when(jnp.logical_not(own))(copies[0].start)
-
-    for g in range(8):
-        start_either(q_copy(g), q_dest(g) == s)
+    def start_either(there, here, own):
+        pl.when(own)(here.start)
+        pl.when(jnp.logical_not(own))(there.start)
+
+    for t in range(2):
+        start_either(*q_copy(t))
 
     def kv_copy(role, g):
         seq, ctx = kv_dest(role, g)
@@ -157,6 +163,9 @@
             pl.when(own)(here.start)
             pl.when(other)(there.start)
 
+    for t in range(2, NB):
+        start_either(*q_copy(t))
+
     def landed(ref, sem):
         pltpu.make_async_copy(ref, ref, sem).wait()
 
@@ -164,13 +173,13 @@
         piece = q_buf.at[n, rows_c]
         return remote(piece, piece, y_send.at[j - 1, n], y_recv.at[j - 1, n], s, (c + j) % CTX)
 
-    def forward(n, _):
+    def forward(n):
         landed(q_buf.at[n, rows_c], q_recv.at[n])
         for j in range(1, CTX):
             y_copy(n, j).start()
-        return 0
-
-    lax.fori_loop(0, NB, forward, 0)
+
+    for u in range(AHEAD):
+        forward(order(u))
 
     landed(tbl_buf, t_recv)
     to_smem = pltpu.make_async_copy(tbl_buf, tbl, smem_sem)
@@ -186,24 +195,30 @@
         return jnp.where(lane % HEADS == h, m + jnp.log2(l), total)
 
     def near(n):
-        @pl.when(n % 2 == 0)
+        @pl.when((n % 2 == 1) == (group == 2 * c + 1))
         def _():
             pl.when(near_b > 0)(lambda: landed(kvn, kv_recv))
             pl.when(near_b == 0)(lambda: landed(kvn.at[pl.ds(KROWS, KROWS)], kv_recv))
 
-        key = lax.broadcasted_iota(jnp.int32, (ROWS, 2 * KROWS), 1)
-        row = lax.broadcasted_iota(jnp.int32, (ROWS, 2 * KROWS), 0)
+        half = HEADS // 2
+        key = lax.broadcasted_iota(jnp.int32, (half * ROWS, 2 * KROWS), 1)
+        row = lax.broadcasted_iota(jnp.int32, (half * ROWS, 2 * KROWS), 0) % ROWS
         first = jnp.where(near_b > 0, 0, KROWS)
         visible = (key >= first) & (key <= row + (KROWS + (n % 2) * ROWS))
         total = jnp.zeros((ROWS, D), F32)
-        for h in range(HEADS):
-            sc = lax.dot_general(q_buf[n, :, h * D:(h + 1) * D], kvn[:, :D], NT, preferred_element_type=F32)
+        for h0 in (0, half):
+            qq = jnp.concatenate([q_buf[n, :, h * D:(h + 1) * D] for h in range(h0, h0 + half)], 0)
+            sc = lax.dot_general(qq, kvn[:, :D], NT, preferred_element_type=F32)
             sc = jnp.where(visible, sc * C, -jnp.inf)
             m = jnp.max(sc, axis=1, keepdims=True)
             p = jnp.exp2(sc - m)
             l = jnp.sum(p, axis=1, keepdims=True)
-            o = jnp.dot(p.astype(BF16), kvn[:, D:], preferred_element_type=F32)
-            total = finish(o, l, m, h, nacc, total)
+            o = jnp.dot(p.astype(BF16), kvn[:, D:], preferred_element_type=F32) * (1.0 / l)
+            logs = m + jnp.log2(l)
+            for h in range(h0, h0 + half):
+                rows = slice((h - h0) * ROWS, (h - h0 + 1) * ROWS)
+                nacc[:, h * D:(h + 1) * D] = o[rows]
+                total = jnp.where(lane % HEADS == h, logs[rows], total)
         nlse[...] = total
 
     def attend(n):
@@ -284,11 +299,14 @@
             cols = slice(h * D, (h + 1) * D)
             o = sum(part[:, cols].astype(F32) * w[:, h:h + 1] for part, w in zip(parts, weights))
             fin[n, :, cols] = o.astype(BF16)
-        start_either(f_copy(n), f_seq(n) == s)
-
-    def step(n, _):
-        @pl.when(n < NB)
+        start_either(*f_copy(n), f_seq(n) == s)
+
+    def step(u, _):
+        pl.when(u < NB - AHEAD)(lambda: forward(order(u + AHEAD)))
+
+        @pl.when(u < NB)
         def _():
+            n = order(u)
             for j in range(1, CTX):
                 rows = pl.ds(pl.multiple_of(((c + CTX - j) % CTX) * PIECE, PIECE), PIECE)
                 landed(q_buf.at[n, rows], y_recv.at[j - 1, n])
@@ -300,7 +318,7 @@
             for j in range(1, CTX):
                 m_copy(n, j).start()
 
-        pl.when(n >= LAG)(lambda: join(n - LAG))
+        pl.when(u >= LAG)(lambda: join(order(u - LAG)))
         return 0
 
     lax.fori_loop(0, NB + LAG, step, 0)
@@ -308,7 +326,8 @@
     for j in range(1, HEADS):
         t_copy(j).wait_send()
     for g in range(8):
-        pl.when(q_dest(g) != s)(q_copy(g)[0].wait_send)
+        there, _, own = q_copy(g)
+        pl.when(jnp.logical_not(own))(there.wait_send)
         for role in range(2):
             there, _, _, other = kv_copy(role, g)
             pl.when(other)(there.wait_send)
@@ -328,13 +347,13 @@
     ids = block_ids[0].transpose(2, 1, 0)
     used = block_counts.transpose(0, 2, 1)
     blocks = cache_keys.shape[1] // KROWS
-    hbm = pl.BlockSpec(memory_space=pl.ANY)
+    hbm = pl.BlockSpec(memory_space=pltpu.MemorySpace.HBM)
     dma = pltpu.SemaphoreType.DMA
     return pl.pallas_call(
         kernel,
         out_shape=jax.ShapeDtypeStruct(queries.shape, BF16),
         in_specs=[hbm] * 7,
-        out_specs=hbm,
+        out_specs=pl.BlockSpec(memory_space=pl.ANY),
         scratch_shapes=[
             pltpu.VMEM((NB, ROWS, WIDE), BF16),
             pltpu.VMEM((blocks, KROWS, D), BF16),

time: 62.5 us -> 52.7 us (0.84)
  the two profiles are of different devices: /device:TPU:7 before, /device:TPU:1 now
where the time goes in v3:
time: 52.7 us; the launch traced here: 52.1 us
  Pallas kernels  50.5 us (96%)
  local copies, waits for them, and re-layouts  1.67 us (3%)
    pallas_call x1, Pallas kernels, body(): pl.pallas_call(kernel, out_shape=jax.ShapeDtypeStruct(queries.shape, BF16...  50.5 us
    unnamed x1, local copies, waits for them, and re-layouts  1.67 us

profile of v3, /device:TPU:1, one launch (start us, length us, event | category | flops | bytes accessed | tf_op | source)
XLA Modules:
  0.0 52.1 jit_solution(6206999306055756853)
XLA Ops:
  0.0 50.5 %attend_all.1 = bf16[16,8192]{1,0:T(8,128)(2,1)} custom-call(bf16[16,8192]{1,0:T(8,128)(2,1)} %q_hbm.1, bf16[16,1024]{1,0:T(8,128)(2,1)} %nk_hbm.1, bf16[16,1024]{1,0:T(8,128)(2,1)} %nv_hbm.1, bf16[64,128,128]{2,1,0:T(8,128)(2,1)} %bitcast.6, bf16[64,128,128]{2,1,0:T(8,128)(2,1)} %bitcast.7, s32[12,1,64]{2,1,0:T(1,128)} %bitcast.8, s32[1,1,64]{2,1,0:T(1,128)} %bitcast.9), custom_call_target="tpu_custom_call" | custom-call | tf_op jit(solution)/shard_map/attend_all/pallas_call | solution.py:352
  50.5 1.7 %copy.9 = bf16[16,8192]{1,0:T(8,128)(2,1)} copy(bf16[16,8192]{1,0:T(8,128)(2,1)} %attend_all.1) | data formatting | bytes 524288

commit v4 on v3

--- a/solution.py
+++ b/solution.py
@@ -19,7 +19,8 @@
 PIECE = ROWS // CTX
 WIDE = HEADS * D
 MSG = WIDE + D
-LAG = 4
+LAG = 5
+NEAR_AT = 3
 AHEAD = 3
 C = math.log2(math.e) / math.sqrt(D)
 NT = (((1,), (1,)), ((), ()))
@@ -39,7 +40,7 @@
 
 def kernel(
     q_hbm, nk_hbm, nv_hbm, k_hbm, v_hbm, ids_hbm, used_hbm, out_hbm,
-    q_buf, k_buf, v_buf, nks, nvs, kvs, kvn, ids, used, own_tbl, tbl_buf, tbl, s_buf, acc, lse, nacc, nlse, msg, rcv, fin,
+    q_buf, k_buf, v_buf, nks, nvs, kvs, kvn, ids, used, own_tbl, tbl_buf, tbl, s_buf, acc, lse, kept, kept_lse, nacc, nlse, msg, rcv, fin,
     load_sem, q_send, q_recv, y_send, y_recv, kv_send, kv_recv, t_send, t_recv, m_send, m_recv, f_send, f_recv, smem_sem,
 ):
     s, c = lax.axis_index("seq"), lax.axis_index("ctx")
@@ -98,8 +99,9 @@
         loads[i].wait()
     own_tbl[...] = jnp.zeros_like(own_tbl)
     for t in range(KQ):
-        own_tbl[t:t + 1, :BLOCKS] = jnp.where(t < used[0], ids[t], ids[0])
-    own_tbl[KQ:KQ + 1, :BLOCKS] = used[0]
+        at = BLOCKS * (t // 8)
+        own_tbl[t % 8:t % 8 + 1, at:at + BLOCKS] = jnp.where(t < used[0], ids[t], ids[0])
+    own_tbl[KQ % 8:KQ % 8 + 1, BLOCKS:] = used[0]
     for g in range(8):
         kvs[g, :, :D] = nks[:, g * D:(g + 1) * D]
         kvs[g, :, D:] = nvs[:, g * D:(g + 1) * D]
@@ -195,11 +197,6 @@
         return jnp.where(lane % HEADS == h, m + jnp.log2(l), total)
 
     def near(n):
-        @pl.when((n % 2 == 1) == (group == 2 * c + 1))
-        def _():
-            pl.when(near_b > 0)(lambda: landed(kvn, kv_recv))
-            pl.when(near_b == 0)(lambda: landed(kvn.at[pl.ds(KROWS, KROWS)], kv_recv))
-
         half = HEADS // 2
         key = lax.broadcasted_iota(jnp.int32, (half * ROWS, 2 * KROWS), 1)
         row = lax.broadcasted_iota(jnp.int32, (half * ROWS, 2 * KROWS), 0) % ROWS
@@ -228,14 +225,14 @@
             qq = q_buf[n, :, h * D:(h + 1) * D]
             m = jnp.full((ROWS, KROWS), -jnp.inf, F32)
             for t in range(0, KQ, 2):
-                kk = jnp.concatenate([k_buf[tbl[h, t + i, block]] for i in range(2)], 0)
+                kk = jnp.concatenate([k_buf[tbl[h, (t + i) % 8, block + BLOCKS * ((t + i) // 8)]] for i in range(2)], 0)
                 sc = lax.dot_general(qq, kk, NT, preferred_element_type=F32)
                 s_buf[h, :, t * KROWS:(t + 2) * KROWS] = sc
                 m = jnp.maximum(m, jnp.maximum(sc[:, :KROWS], sc[:, KROWS:]))
             tops.append(jnp.max(m, axis=1, keepdims=True) * C)
         total = jnp.zeros((ROWS, D), F32)
         for h in range(HEADS):
-            count, m = tbl[h, KQ, block], tops[h]
+            count, m = tbl[h, KQ % 8, block + BLOCKS], tops[h]
             o = jnp.zeros((ROWS, D), F32)
             l = jnp.zeros((ROWS, KROWS), F32)
             for t in range(0, KQ, 2):
@@ -245,7 +242,7 @@
                     p = jnp.exp2(s_buf[h, :, (t + i) * KROWS:(t + i + 1) * KROWS] * C - shift)
                     l = l + p
                     parts.append(p.astype(BF16))
-                vv = jnp.concatenate([v_buf[tbl[h, t + i, block]] for i in range(2)], 0)
+                vv = jnp.concatenate([v_buf[tbl[h, (t + i) % 8, block + BLOCKS * ((t + i) // 8)]] for i in range(2)], 0)
                 o = o + jnp.dot(jnp.concatenate(parts, 1), vv, preferred_element_type=F32)
             total = finish(o, jnp.sum(l, axis=1, keepdims=True), m, h, acc, total)
         lse[...] = total
@@ -301,7 +298,31 @@
             fin[n, :, cols] = o.astype(BF16)
         start_either(*f_copy(n), f_seq(n) == s)
 
+    def send_parts(n):
+        pack(n)
+        for j in (2, 1, 3):
+            m_copy(n, j).start()
+
+    def kept_near(k, _):
+        n = 2 * c + k
+
+        @pl.when((n + NB - group) % NB < NEAR_AT)
+        def _():
+            acc[...] = kept[k]
+            lse[...] = kept_lse[k]
+            near(n)
+            merge_near()
+            send_parts(n)
+
+        return 0
+
     def step(u, _):
+        @pl.when(u == NEAR_AT)
+        def _():
+            pl.when(near_b > 0)(lambda: landed(kvn, kv_recv))
+            pl.when(near_b == 0)(lambda: landed(kvn.at[pl.ds(KROWS, KROWS)], kv_recv))
+            lax.fori_loop(0, 2, kept_near, 0)
+
         pl.when(u < NB - AHEAD)(lambda: forward(order(u + AHEAD)))
 
         @pl.when(u < NB)
@@ -311,12 +332,20 @@
                 rows = pl.ds(pl.multiple_of(((c + CTX - j) % CTX) * PIECE, PIECE), PIECE)
                 landed(q_buf.at[n, rows], y_recv.at[j - 1, n])
             is_near = n // 2 == c
-            pl.when(is_near)(lambda: near(n))
+            later = is_near & (u < NEAR_AT)
             attend(n)
-            pl.when(is_near)(merge_near)
-            pack(n)
-            for j in range(1, CTX):
-                m_copy(n, j).start()
+
+            @pl.when(later)
+            def _():
+                kept[n % 2] = acc[...]
+                kept_lse[n % 2] = lse[...]
+
+            @pl.when(is_near & jnp.logical_not(later))
+            def _():
+                near(n)
+                merge_near()
+
+            pl.when(jnp.logical_not(later))(lambda: send_parts(n))
 
         pl.when(u >= LAG)(lambda: join(order(u - LAG)))
         return 0
@@ -364,12 +393,14 @@
             pltpu.VMEM((2 * KROWS, 2 * D), BF16),
             pltpu.VMEM(ids.shape, jnp.int32),
             pltpu.VMEM(used.shape, jnp.int32),
-            pltpu.VMEM((16, D), jnp.int32),
-            pltpu.VMEM((HEADS, 16, D), jnp.int32),
-            pltpu.SMEM((HEADS, 16, D), jnp.int32),
+            pltpu.VMEM((8, D), jnp.int32),
+            pltpu.VMEM((HEADS, 8, D), jnp.int32),
+            pltpu.SMEM((HEADS, 8, D), jnp.int32),
             pltpu.VMEM((HEADS, ROWS, KQ * KROWS), F32),
             pltpu.VMEM((ROWS, WIDE), F32),
             pltpu.VMEM((ROWS, D), F32),
+            pltpu.VMEM((2, ROWS, WIDE), F32),
+            pltpu.VMEM((2, ROWS, D), F32),
             pltpu.VMEM((ROWS, WIDE), F32),
             pltpu.VMEM((ROWS, D), F32),
             pltpu.VMEM((NB, ROWS, MSG), BF16),

time: 52.7 us -> 51.9 us (0.985)
  no operation moved by 1% of the time
where the time goes in v4:
time: 51.9 us; the launch traced here: 51.7 us
  Pallas kernels  50.1 us (97%)
  local copies, waits for them, and re-layouts  1.67 us (3%)
    pallas_call x1, Pallas kernels, body(): pl.pallas_call(kernel, out_shape=jax.ShapeDtypeStruct(queries.shape, BF16...  50.1 us
    unnamed x1, local copies, waits for them, and re-layouts  1.67 us

profile of v4, /device:TPU:1, one launch (start us, length us, event | category | flops | bytes accessed | tf_op | source)
XLA Modules:
  0.0 51.7 jit_solution(11144353454430676400)
XLA Ops:
  0.0 50.1 %attend_all.1 = bf16[16,8192]{1,0:T(8,128)(2,1)} custom-call(bf16[16,8192]{1,0:T(8,128)(2,1)} %q_hbm.1, bf16[16,1024]{1,0:T(8,128)(2,1)} %nk_hbm.1, bf16[16,1024]{1,0:T(8,128)(2,1)} %nv_hbm.1, bf16[64,128,128]{2,1,0:T(8,128)(2,1)} %bitcast.6, bf16[64,128,128]{2,1,0:T(8,128)(2,1)} %bitcast.7, s32[12,1,64]{2,1,0:T(1,128)} %bitcast.8, s32[1,1,64]{2,1,0:T(1,128)} %bitcast.9), custom_call_target="tpu_custom_call" | custom-call | tf_op jit(solution)/shard_map/attend_all/pallas_call | solution.py:381
  50.1 1.7 %copy.9 = bf16[16,8192]{1,0:T(8,128)(2,1)} copy(bf16[16,8192]{1,0:T(8,128)(2,1)} %attend_all.1) | data formatting | bytes 524288

commit v5 on v4

--- a/solution.py
+++ b/solution.py
@@ -316,6 +316,10 @@
 
         return 0
 
+    def join_at(i, _):
+        join(order(i))
+        return 0
+
     def step(u, _):
         @pl.when(u == NEAR_AT)
         def _():
@@ -347,10 +351,15 @@
 
             pl.when(jnp.logical_not(later))(lambda: send_parts(n))
 
-        pl.when(u >= LAG)(lambda: join(order(u - LAG)))
+        first = u - LAG + jnp.where(u >= NB, 1, 0)
+
+        @pl.when(u >= LAG)
+        def _():
+            lax.fori_loop(first, first + jnp.where(u == NB - 1, 2, 1), join_at, 0)
+
         return 0
 
-    lax.fori_loop(0, NB + LAG, step, 0)
+    lax.fori_loop(0, NB + LAG - 1, step, 0)
 
     for j in range(1, HEADS):
         t_copy(j).wait_send()

time: 51.9 us -> 51.9 us (level)
  no operation moved by 1% of the time
where the time goes in v5:
time: 51.9 us; the launch traced here: 51.7 us
  Pallas kernels  50.1 us (97%)
  local copies, waits for them, and re-layouts  1.67 us (3%)
    pallas_call x1, Pallas kernels, body(): pl.pallas_call(kernel, out_shape=jax.ShapeDtypeStruct(queries.shape, BF16...  50.1 us
    unnamed x1, local copies, waits for them, and re-layouts  1.67 us

profile of v5, /device:TPU:1, one launch (start us, length us, event | category | flops | bytes accessed | tf_op | source)
XLA Modules:
  0.0 51.7 jit_solution(17491264531735203478)
XLA Ops:
  0.0 50.1 %attend_all.1 = bf16[16,8192]{1,0:T(8,128)(2,1)} custom-call(bf16[16,8192]{1,0:T(8,128)(2,1)} %q_hbm.1, bf16[16,1024]{1,0:T(8,128)(2,1)} %nk_hbm.1, bf16[16,1024]{1,0:T(8,128)(2,1)} %nv_hbm.1, bf16[64,128,128]{2,1,0:T(8,128)(2,1)} %bitcast.6, bf16[64,128,128]{2,1,0:T(8,128)(2,1)} %bitcast.7, s32[12,1,64]{2,1,0:T(1,128)} %bitcast.8, s32[1,1,64]{2,1,0:T(1,128)} %bitcast.9), custom_call_target="tpu_custom_call" | custom-call | tf_op jit(solution)/shard_map/attend_all/pallas_call | solution.py:390
  50.1 1.7 %copy.9 = bf16[16,8192]{1,0:T(8,128)(2,1)} copy(bf16[16,8192]{1,0:T(8,128)(2,1)} %attend_all.1) | data formatting | bytes 524288
